TPU v7x, 256 devices: a whole 4x4x8 slice. The times are simulated.
256 devices in a mesh: leaf: 16 (over y, x), sep: 8 (over z), mode: 2 (over core).
Axes of the slice: x: 4, y: 4, z: 8, core: 2. Of those that a mesh axis runs over, the one named last changes fastest.
Arguments:
- modes: bfloat16 [1024, 2048, 256], P(('leaf', 'sep'), 'mode'), may hold values from -0.125 to 0.125
- coupling: bfloat16 [1024, 2048, 256], P(('leaf', 'sep'), 'mode'), may hold values from -6 to 6
- eigenvalues: float32 [1024, 256], P(('leaf', 'sep'), 'mode'), may hold values from 200 to 4000
- separator_of: int32 [1024, 1], P(('leaf', 'sep')), may hold values from 0 to 7; in each aligned block of 8 rows (0 to 7, 8 to 15, ...) at most 2 rows name the same one
- row_offset: int32 [1024], P(('leaf', 'sep')), may hold values from 0 to 256
- stiffness: bfloat16 [8, 512, 512], P('sep', None, ('leaf', 'mode')), may hold values from -1 to 40
- start_block: bfloat16 [8, 512, 256], P('sep', ('leaf', 'mode')), may hold values from -40 to 40
- rotations: bfloat16 [8, 2, 256, 256], P('sep'), may hold values from -0.375 to 0.375
Outputs:
- subspace: bfloat16 [8, 512, 256], P('sep', ('leaf', 'mode'))
- column_norms: float32 [8, 2, 256], P('sep')
Inputs may be any that keep to these rules, and one draw needn't show every extreme that they name: `separator_of`: among the 8 leaves of one device at most 2 couple to one separator, and in every draw some separator gets exactly 2 of them.
All inputs are finite; a program needn't handle non-finite values.
Results may differ from a plain program's by a relative error of at most 0.0075.
Values may be sent and summed in bfloat16 or wider, within the bound.
No kernel may reach another device: no remote copies, remote signals or barrier semaphores. Data moves between devices by JAX's collectives and lax.ppermute only.
A program may use at most 64 MiB of HBM per device.

v0:
```python
import jax
import jax.numpy as jnp
from jax import lax
from jax.sharding import PartitionSpec as P

SEP_ROWS = 512
CAP = 2
ITERS = 2
epsilon = 1e-06


def leaf_projection(modes, coupling, eigenvalues):
    summed = lax.psum_scatter(
        jnp.einsum("ldm,ldw->mlw", modes, coupling, preferred_element_type=jnp.float32),
        "mode",
        scatter_dimension=0,
        tiled=True,
    )
    return (summed / jnp.sqrt(eigenvalues.T)[:, :, None]).astype(jnp.bfloat16)


def route_blocks(scaled, separator_of, row_offset):
    groups = lax.axis_size("sep")
    leaves = scaled.shape[1]
    target = separator_of[:, 0]
    leaf_order = jnp.arange(leaves)
    earlier = (target[:, None] == target[None, :]) & (leaf_order[None, :] < leaf_order[:, None])
    position = jnp.sum(earlier.astype(jnp.int32), 1)
    slot_of = target * CAP + position
    slot_table = slot_of[None, :] == jnp.arange(groups * CAP)[:, None]
    send_blocks = jnp.einsum(
        "sl,mlw->smw", slot_table.astype(jnp.bfloat16), scaled, preferred_element_type=jnp.float32
    ).astype(jnp.bfloat16)
    send_offsets = jnp.sum(jnp.where(slot_table, row_offset[None, :], 0), 1)
    block_shape = (groups, CAP, send_blocks.shape[1], send_blocks.shape[2])
    got_blocks, got_offsets = (
        lax.all_to_all(
            send_blocks.reshape(block_shape), "sep", split_axis=0, concat_axis=0, tiled=True
        ),
        lax.all_to_all(
            send_offsets.reshape(groups, CAP), "sep", split_axis=0, concat_axis=0, tiled=True
        ),
    )
    return (
        got_blocks.reshape(groups * CAP, block_shape[2], block_shape[3]),
        got_offsets.reshape(groups * CAP),
    )


def coupled_correction(full_block, blocks, offsets):
    width_rows = blocks.shape[2]

    def add_slot(slot_index, accumulated):
        offset = offsets[slot_index]
        weights = blocks[slot_index]
        window = lax.dynamic_slice_in_dim(full_block, offset, width_rows, 0)
        projected = jnp.dot(weights, window, preferred_element_type=jnp.float32).astype(
            jnp.bfloat16
        )
        update = jnp.einsum("mw,mc->wc", weights, projected, preferred_element_type=jnp.float32)
        current = lax.dynamic_slice_in_dim(accumulated, offset, width_rows, 0)
        return lax.dynamic_update_slice_in_dim(accumulated, current + update, offset, 0)

    initial = jnp.zeros(full_block.shape, jnp.float32)
    return lax.fori_loop(0, blocks.shape[0], add_slot, initial)


def gather_rows(own_block):
    return lax.all_gather(own_block, ("leaf", "mode"), axis=0, tiled=True)


def per_device(
    modes, coupling, eigenvalues, separator_of, row_offset, stiffness, start_block, rotations
):
    scaled = leaf_projection(modes, coupling, eigenvalues)
    blocks, offsets = route_blocks(scaled, separator_of, row_offset)
    stiff_columns = stiffness[0]
    own_block = start_block[0]
    ritz_turns = rotations[0]
    own_rows = own_block.shape[0]
    norm_list = []
    for iteration in range(ITERS):
        full_block = gather_rows(own_block)
        correction = coupled_correction(full_block, blocks, offsets)

        def assemble_rows(first_row, row_count, block_now=own_block, correction_now=correction):
            product = jnp.dot(stiff_columns, block_now, preferred_element_type=jnp.float32)
            return product - correction_now

        summed = lax.psum_scatter(
            assemble_rows(jnp.int32(0), lax.axis_size(("leaf", "mode")) * own_rows),
            ("leaf", "mode"),
            scatter_dimension=0,
            tiled=True,
        )
        squares = lax.psum(jnp.sum(summed * summed, 0), ("leaf", "mode"))
        column_scale = jnp.sqrt(squares / SEP_ROWS + epsilon)
        normed = (summed / column_scale).astype(jnp.bfloat16)
        own_block = jnp.dot(
            normed, ritz_turns[iteration], preferred_element_type=jnp.float32
        ).astype(jnp.bfloat16)
        norm_list.append(column_scale)
    return (own_block[None], jnp.stack(norm_list)[None])


def solution(mesh):
    in_specs = (
        P(("leaf", "sep"), "mode", None),
        P(("leaf", "sep"), "mode", None),
        P(("leaf", "sep"), "mode"),
        P(("leaf", "sep"), None),
        P(("leaf", "sep")),
        P("sep", None, ("leaf", "mode")),
        P("sep", ("leaf", "mode"), None),
        P("sep", None, None, None),
    )
    out_specs = (P("sep", ("leaf", "mode"), None), P("sep", None, None))
    return jax.shard_map(
        per_device, mesh=mesh, in_specs=in_specs, out_specs=out_specs, check_vma=False
    )
```

profile of v0, /device:TPU:1, one launch (start us, length us, event | category | flops | bytes accessed | tf_op | source)
XLA Modules:
  0.0 560.8 jit_solution(13401757239637969915)
XLA Ops:
  7.3 6.2 %convolution_bitcast_fusion = f32[256,8,256]{0,2,1:T(8,128)} fusion(bf16[8,1024,256]{2,1,0:T(8,128)(2,1)} %param.13, bf16[8,1024,256]{2,1,0:T(8,128)(2,1)} %param.12), kind=kOutput, calls=%fused_computation.13 | convolution fusion | flops 1073741824 | bytes 10485760 | tf_op jit(solution)/shard_map/ldm,ldw->mlw/dot_general | solution.py:14
  13.8 0.7 all_to_all.9
  14.5 9.0 %all-to-all-start = ((s32[8,1,2]{2,1,0:T(1,128)}), s32[8,1,2]{2,1,0:T(1,128)S(1)}, u32[]{:S(2)}, u32[]{:S(2)}) async-start(s32[8,1,2]{2,1,0:T(1,128)} %bitcast.7), calls=%async_computation | async-start | bytes 8192 | tf_op jit(solution)/shard_map/all_to_all | solution.py:40
  23.5 9.3 %reduce-scatter.6.cloned.1.call-done = f32[128,8,256]{0,2,1:T(8,128)} async-done(((f32[256,8,256]{0,2,1:T(8,128)}), f32[128,8,256]{0,2,1:T(8,128)}) %reduce-scatter.6.cloned.1.call-update) | async-done | bytes 1048592 | tf_op jit(solution)/shard_map/reduce_scatter | solution.py:13
  32.8 1.3 divide_convert_fusion
  35.5 1.8 copy.30
  37.3 6.8 %all-to-all-start.1 = ((bf16[8,2,128,256]{3,1,2,0:T(2,128)(2,1)}), bf16[8,2,128,256]{3,1,2,0:T(2,128)(2,1)S(1)}, u32[]{:S(2)}, u32[]{:S(2)}) async-start(bf16[8,2,128,256]{3,1,2,0:T(2,128)(2,1)} %copy.30), calls=%async_computation.2 | async-start | bytes 2097152 | tf_op jit(solution)/shard_map/all_to_all | solution.py:37
  44.2 25.3 %all-gather = bf16[1,512,256]{2,1,0:T(8,128)(2,1)S(1)} all-gather(bf16[1,16,256]{2,1,0:T(8,128)(2,1)S(1)} %copy-done.1), channel_id=2, replica_groups=mesh['leaf'=16,'sep'=8,'mode'=2] {'leaf','mode'}, dimensions={1}, use_global_device_ids=true | all-gather | bytes 270336 | tf_op jit(solution)/shard_map/all_gather | solution.py:69
  70.0 0.7 reduce.3
  70.8 2.6 all-to-all-done.1
  73.6 74.0 %while.26 = (s32[]{:T(128)}, f32[512,256]{1,0:T(8,128)S(1)}, s32[16]{0:T(128)S(1)}, bf16[16,128,256]{2,1,0:T(8,128)(2,1)S(1)}, bf16[512,256]{1,0:T(8,128)(2,1)S(1)}, /*index=5*/s32[]{:T(128)}, s32[]{:T(128)}, s32[]{:T(128)}) while((s32[]{:T(128)}, f32[512,256]{1,0:T(8,128)S(1)}, s32[16]{0:T(128)S(1)}, bf16[16,128,256]{2,1,0:T(8,128)(2,1)S(1)}, ...), condition=%wide.region_4.5_spmd, body=%wide.region_3.4_spmd.sunk | while | flops 33652740 | bytes 1312903 | solution.py:65
  73.6 0.6 dynamic_slice.92
  76.5 1.1 dynamic_update_slice.16
  77.7 0.6 dynamic_slice.92
  80.6 1.9 dynamic_update_slice.16
  82.5 0.6 dynamic_slice.92
  85.4 1.9 dynamic_update_slice.16
  87.3 0.6 dynamic_slice.92
  90.2 1.9 dynamic_update_slice.16
  92.1 0.6 dynamic_slice.92
  95.0 1.3 dynamic_update_slice.16
  96.3 0.6 dynamic_slice.92
  99.3 1.9 dynamic_update_slice.16
  101.2 0.6 dynamic_slice.92
  104.1 1.9 dynamic_update_slice.16
  108.9 1.9 dynamic_update_slice.16
  113.7 1.1 dynamic_update_slice.16
  114.9 0.6 dynamic_slice.92
  117.8 1.9 dynamic_update_slice.16
  119.7 0.6 dynamic_slice.92
  122.6 1.8 dynamic_update_slice.16
  127.4 1.9 dynamic_update_slice.16
  132.2 1.1 dynamic_update_slice.16
  136.3 1.9 dynamic_update_slice.16
  141.1 1.7 dynamic_update_slice.16
  145.7 1.9 dynamic_update_slice.16
  147.7 1.1 convolution_subtract_fusion
  148.8 80.6 %reduce-scatter.8.cloned.1.call-done = f32[16,256]{1,0:T(8,128)} async-done(((f32[512,256]{1,0:T(8,128)}), f32[16,256]{1,0:T(8,128)}) %reduce-scatter.8.cloned.1.call-update) | async-done | bytes 16400 | tf_op jit(solution)/shard_map/reduce_scatter | solution.py:90
  229.4 0.7 multiply_reduce_fusion.1
  230.1 64.6 %psum.14 = f32[256]{0:T(256)S(1)} all-reduce(f32[256]{0:T(256)S(1)} %multiply_reduce_fusion.1), channel_id=1, replica_groups=mesh['leaf'=16,'sep'=8,'mode'=2] {'leaf','mode'}, use_global_device_ids=true, to_apply=%region_7.8 | all-reduce | flops 256 | bytes 2048 | tf_op jit(solution)/shard_map/psum | solution.py:96
  294.7 0.9 convolution_convert_fusion.4
  295.6 22.6 %all_gather.7 = bf16[512,256]{1,0:T(8,128)(2,1)S(1)} all-gather(bf16[16,256]{1,0:T(8,128)(2,1)S(1)} %convolution_convert_fusion.4), channel_id=1, replica_groups=mesh['leaf'=16,'sep'=8,'mode'=2] {'leaf','mode'}, dimensions={0}, use_global_device_ids=true | all-gather | bytes 270336 | tf_op jit(solution)/shard_map/all_gather | solution.py:69
  318.3 85.1 %while.27 = (s32[]{:T(128)}, f32[512,256]{0,1:T(8,128)S(1)}, s32[16]{0:T(128)S(1)}, bf16[16,128,256]{2,1,0:T(8,128)(2,1)S(1)}, bf16[512,256]{1,0:T(8,128)(2,1)S(1)}, /*index=5*/s32[]{:T(128)}, s32[]{:T(128)}, s32[]{:T(128)}) while((s32[]{:T(128)}, f32[512,256]{0,1:T(8,128)S(1)}, s32[16]{0:T(128)S(1)}, bf16[16,128,256]{2,1,0:T(8,128)(2,1)S(1)}, ...), condition=%wide.region_9.10_spmd, body=%wide.region_8.9_spmd.sunk | while | flops 33652740 | bytes 2884751 | solution.py:65
  321.6 1.8 dynamic_update_slice.17
  326.8 1.9 dynamic_update_slice.17
  332.1 1.9 dynamic_update_slice.17
  337.4 1.9 dynamic_update_slice.17
  342.7 1.8 dynamic_update_slice.17
  347.9 1.9 dynamic_update_slice.17
  353.1 2.2 dynamic_update_slice.17
  358.7 1.9 dynamic_update_slice.17
  364.0 1.8 dynamic_update_slice.17
  369.2 1.9 dynamic_update_slice.17
  374.5 2.2 dynamic_update_slice.17
  380.1 1.9 dynamic_update_slice.17
  385.4 1.8 dynamic_update_slice.17
  390.6 1.9 dynamic_update_slice.17
  395.8 2.2 dynamic_update_slice.17
  401.4 1.9 dynamic_update_slice.17
  403.6 1.0 copy.34
  404.7 82.7 %reduce-scatter.10.cloned.1.call-done = f32[16,256]{1,0:T(8,128)} async-done(((f32[512,256]{1,0:T(8,128)}), f32[16,256]{1,0:T(8,128)}) %reduce-scatter.10.cloned.1.call-update) | async-done | bytes 16400
  487.3 0.8 copy.35
  488.2 64.6 %psum.15 = f32[256]{0:T(256)S(1)} all-reduce(f32[256]{0:T(256)S(1)} %multiply_reduce_fusion), channel_id=1, replica_groups=mesh['leaf'=16,'sep'=8,'mode'=2] {'leaf','mode'}, use_global_device_ids=true, to_apply=%region_12.13 | all-reduce | flops 256 | bytes 2048 | tf_op jit(solution)/shard_map/psum | solution.py:96
  552.8 0.9 fusion.17
  (139 shorter events, 35.4 us)
Async XLA Ops:
  7.2 140.5 %copy-start = (bf16[1,512,16]{1,2,0:T(8,128)(2,1)S(1)}, bf16[1,512,16]{1,2,0:T(8,128)(2,1)}, u32[]{:S(2)}) copy-start(bf16[1,512,16]{1,2,0:T(8,128)(2,1)} %param.17) | copy-start | bytes 49156
  7.2 6.3 %copy-start.4 = (s32[8,1]{0,1:T(1,128)S(1)}, s32[8,1]{0,1:T(1,128)}, u32[]{:S(2)}) copy-start(s32[8,1]{0,1:T(1,128)} %param.15) | copy-start | bytes 100
  7.2 6.5 %copy-start.5 = (s32[8]{0:T(128)S(1)}, s32[8]{0:T(128)}, u32[]{:S(2)}) copy-start(s32[8]{0:T(128)} %param.16) | copy-start | bytes 100
  7.2 16.3 %copy-start.2 = (f32[8,128]{1,0:T(8,128)S(1)}, f32[8,128]{1,0:T(8,128)}, u32[]{:S(2)}) copy-start(f32[8,128]{1,0:T(8,128)} %param.14) | copy-start | bytes 12292
  7.2 25.6 %reduce-scatter.6.cloned.1.call-start = ((), (), s32[]{:S(2)}) async-start(), calls=%async_computation.5 | async-start | bytes 3145728 | tf_op jit(solution)/shard_map/reduce_scatter | solution.py:13
  14.5 22.9 %all-to-all-start = ((s32[8,1,2]{2,1,0:T(1,128)}), s32[8,1,2]{2,1,0:T(1,128)S(1)}, u32[]{:S(2)}, u32[]{:S(2)}) async-start(s32[8,1,2]{2,1,0:T(1,128)} %bitcast.7), calls=%async_computation | async-start | bytes 8192 | tf_op jit(solution)/shard_map/all_to_all | solution.py:40
  34.5 9.6 %copy-start.1 = (bf16[1,16,256]{2,1,0:T(8,128)(2,1)S(1)}, bf16[1,16,256]{2,1,0:T(8,128)(2,1)}, u32[]{:S(2)}) copy-start(bf16[1,16,256]{2,1,0:T(8,128)(2,1)} %param.18) | copy-start | bytes 24580
  37.3 36.0 %all-to-all-start.1 = ((bf16[8,2,128,256]{3,1,2,0:T(2,128)(2,1)}), bf16[8,2,128,256]{3,1,2,0:T(2,128)(2,1)S(1)}, u32[]{:S(2)}, u32[]{:S(2)}) async-start(bf16[8,2,128,256]{3,1,2,0:T(2,128)(2,1)} %copy.30), calls=%async_computation.2 | async-start | bytes 2097152 | tf_op jit(solution)/shard_map/all_to_all | solution.py:37
  44.1 185.3 %reduce-scatter.8.cloned.1.call-start = ((), (), s32[]{:S(2)}) async-start(), calls=%async_computation.6 | async-start | bytes 540672 | tf_op jit(solution)/shard_map/reduce_scatter | solution.py:90
  73.6 221.1 %copy-start.3 = (bf16[1,2,256,256]{3,2,1,0:T(8,128)(2,1)S(1)}, bf16[1,2,256,256]{3,2,1,0:T(8,128)(2,1)}, u32[]{:S(2)}) copy-start(bf16[1,2,256,256]{3,2,1,0:T(8,128)(2,1)} %param.19) | copy-start | bytes 786436
  148.7 338.6 %reduce-scatter.10.cloned.1.call-start = ((), (), s32[]{:S(2)}) async-start(), calls=%async_computation.7 | async-start | bytes 540672
Sparse Core Ops, SparseCore 0:
  13.6 19.1 reduce-scatter.5
  148.9 80.5 reduce-scatter.7
  404.8 82.4 reduce-scatter.9
where the time goes:
time: 562 us; the launch traced here: 561 us
  blocking collectives  177 us (31%)
  waiting for transfers between devices  175 us (31%)
  local copies, waits for them, and re-layouts  89.7 us (16%)
  loops' own time  63.5 us (11%)
  matrix products  21.7 us (4%)
  starting transfers between devices  15.9 us (3%)
  between operations  13.9 us (2%)
    psum x2, blocking collectives, per_device(): squares = lax.psum(jnp.sum(summed * summed, 0), ('leaf', 'mode'))  129 us
    unnamed x4, waiting for transfers between devices  82.7 us
    reduce_scatter x1, waiting for transfers between devices, per_device(): lax.psum_scatter(assemble_rows(jnp.int32(0), lax.axis_size(('leaf', 'mode...  80.6 us
    another operation x2, loops' own time, coupled_correction(): return lax.fori_loop(0, blocks.shape[0], add_slot, initial)  63.5 us
    dynamic_update_slice x48, local copies, waits for them, and re-layouts, add_slot(): lax.dynamic_update_slice_in_dim(accumulated, current + update, offset, 0)  60.6 us
    all_gather x2, blocking collectives, gather_rows(): return lax.all_gather(own_block, ('leaf', 'mode'), axis=0, tiled=True)  48 us
    dynamic_slice x32, local copies, waits for them, and re-layouts, add_slot(): offset = offsets[slot_index]  18.8 us
    dot_general x32, matrix products, add_slot(): jnp.einsum('mw,mc->wc', weights, projected, preferred_element_type=jnp.fl...  11.9 us
  transfers between devices with their start and end apart: 5, of which 4 were waited for; matrix products, arithmetic and copies ran while one was open for 1% of the time, Pallas kernels for 0%

commit v1 on v0

--- a/solution.py
+++ b/solution.py
@@ -93,7 +93,7 @@
             scatter_dimension=0,
             tiled=True,
         )
-        squares = lax.psum(jnp.sum(summed * summed, 0), ("leaf", "mode"))
+        squares = jnp.sum(lax.all_gather(jnp.sum(summed * summed, 0), ("leaf", "mode")), axis=0)
         column_scale = jnp.sqrt(squares / SEP_ROWS + epsilon)
         normed = (summed / column_scale).astype(jnp.bfloat16)
         own_block = jnp.dot(

time: 562 us -> 484 us (0.86)
  blocking collectives: 177 us -> 99.9 us
    psum x2 -> x0, blocking collectives: 129 us -> none  [per_device(): squares = lax.psum(jnp.sum(summed * summed, 0), ('leaf', 'mode'))]
    all_gather x0 -> x2, blocking collectives: none -> 51.9 us  [per_device(): lax.all_gather(jnp.sum(summed * summed, 0), ('leaf', 'mode'))]
where the time goes in v1:
time: 484 us; the launch traced here: 483 us
  waiting for transfers between devices  175 us (36%)
  blocking collectives  99.9 us (21%)
  local copies, waits for them, and re-layouts  89.7 us (19%)
  loops' own time  63.5 us (13%)
  matrix products  21.7 us (4%)
  starting transfers between devices  15.9 us (3%)
  between operations  13.9 us (3%)
    unnamed x4, waiting for transfers between devices  82 us
    reduce_scatter x1, waiting for transfers between devices, per_device(): lax.psum_scatter(assemble_rows(jnp.int32(0), lax.axis_size(('leaf', 'mode...  80.6 us
    another operation x2, loops' own time, coupled_correction(): return lax.fori_loop(0, blocks.shape[0], add_slot, initial)  63.5 us
    dynamic_update_slice x48, local copies, waits for them, and re-layouts, add_slot(): lax.dynamic_update_slice_in_dim(accumulated, current + update, offset, 0)  60.6 us
    all_gather x2, blocking collectives, per_device(): lax.all_gather(jnp.sum(summed * summed, 0), ('leaf', 'mode'))  51.9 us
    all_gather x2, blocking collectives, gather_rows(): return lax.all_gather(own_block, ('leaf', 'mode'), axis=0, tiled=True)  48 us
    dynamic_slice x32, local copies, waits for them, and re-layouts, add_slot(): offset = offsets[slot_index]  18.8 us
    dot_general x32, matrix products, add_slot(): jnp.einsum('mw,mc->wc', weights, projected, preferred_element_type=jnp.fl...  11.9 us
  transfers between devices with their start and end apart: 5, of which 4 were waited for; matrix products, arithmetic and copies ran while one was open for 1% of the time, Pallas kernels for 0%

profile of v1, /device:TPU:1, one launch (start us, length us, event | category | flops | bytes accessed | tf_op | source)
XLA Modules:
  0.0 483.0 jit_solution(13514919044863120218)
XLA Ops:
  7.3 6.2 %convolution_bitcast_fusion = f32[256,8,256]{0,2,1:T(8,128)} fusion(bf16[8,1024,256]{2,1,0:T(8,128)(2,1)} %param.13, bf16[8,1024,256]{2,1,0:T(8,128)(2,1)} %param.12), kind=kOutput, calls=%fused_computation.13 | convolution fusion | flops 1073741824 | bytes 10485760 | tf_op jit(solution)/shard_map/ldm,ldw->mlw/dot_general | solution.py:14
  13.8 0.7 all_to_all.9
  14.5 9.0 %all-to-all-start = ((s32[8,1,2]{2,1,0:T(1,128)}), s32[8,1,2]{2,1,0:T(1,128)S(1)}, u32[]{:S(2)}, u32[]{:S(2)}) async-start(s32[8,1,2]{2,1,0:T(1,128)} %bitcast.7), calls=%async_computation | async-start | bytes 8192 | tf_op jit(solution)/shard_map/all_to_all | solution.py:40
  23.5 9.3 %reduce-scatter.6.cloned.1.call-done = f32[128,8,256]{0,2,1:T(8,128)} async-done(((f32[256,8,256]{0,2,1:T(8,128)}), f32[128,8,256]{0,2,1:T(8,128)}) %reduce-scatter.6.cloned.1.call-update) | async-done | bytes 1048592 | tf_op jit(solution)/shard_map/reduce_scatter | solution.py:13
  32.8 1.3 divide_convert_fusion
  35.5 1.8 copy.30
  37.3 6.8 %all-to-all-start.1 = ((bf16[8,2,128,256]{3,1,2,0:T(2,128)(2,1)}), bf16[8,2,128,256]{3,1,2,0:T(2,128)(2,1)S(1)}, u32[]{:S(2)}, u32[]{:S(2)}) async-start(bf16[8,2,128,256]{3,1,2,0:T(2,128)(2,1)} %copy.30), calls=%async_computation.2 | async-start | bytes 2097152 | tf_op jit(solution)/shard_map/all_to_all | solution.py:37
  44.2 25.3 %all-gather = bf16[1,512,256]{2,1,0:T(8,128)(2,1)S(1)} all-gather(bf16[1,16,256]{2,1,0:T(8,128)(2,1)S(1)} %copy-done.1), channel_id=2, replica_groups=mesh['leaf'=16,'sep'=8,'mode'=2] {'leaf','mode'}, dimensions={1}, use_global_device_ids=true | all-gather | bytes 270336 | tf_op jit(solution)/shard_map/all_gather | solution.py:69
  70.0 0.7 reduce.5
  70.8 2.6 all-to-all-done.1
  73.6 74.0 %while.26 = (s32[]{:T(128)}, f32[512,256]{1,0:T(8,128)S(1)}, s32[16]{0:T(128)S(1)}, bf16[16,128,256]{2,1,0:T(8,128)(2,1)S(1)}, bf16[512,256]{1,0:T(8,128)(2,1)S(1)}, /*index=5*/s32[]{:T(128)}, s32[]{:T(128)}, s32[]{:T(128)}) while((s32[]{:T(128)}, f32[512,256]{1,0:T(8,128)S(1)}, s32[16]{0:T(128)S(1)}, bf16[16,128,256]{2,1,0:T(8,128)(2,1)S(1)}, ...), condition=%wide.region_4.5_spmd, body=%wide.region_3.4_spmd.sunk | while | flops 33652740 | bytes 1312903 | solution.py:65
  73.6 0.6 dynamic_slice.92
  76.5 1.1 dynamic_update_slice.16
  77.7 0.6 dynamic_slice.92
  80.6 1.9 dynamic_update_slice.16
  82.5 0.6 dynamic_slice.92
  85.4 1.9 dynamic_update_slice.16
  87.3 0.6 dynamic_slice.92
  90.2 1.9 dynamic_update_slice.16
  92.1 0.6 dynamic_slice.92
  95.0 1.3 dynamic_update_slice.16
  96.3 0.6 dynamic_slice.92
  99.3 1.9 dynamic_update_slice.16
  101.2 0.6 dynamic_slice.92
  104.1 1.9 dynamic_update_slice.16
  108.9 1.9 dynamic_update_slice.16
  113.7 1.1 dynamic_update_slice.16
  114.9 0.6 dynamic_slice.92
  117.8 1.9 dynamic_update_slice.16
  119.7 0.6 dynamic_slice.92
  122.6 1.8 dynamic_update_slice.16
  127.4 1.9 dynamic_update_slice.16
  132.2 1.1 dynamic_update_slice.16
  136.3 1.9 dynamic_update_slice.16
  141.1 1.7 dynamic_update_slice.16
  145.7 1.9 dynamic_update_slice.16
  147.7 1.1 convolution_subtract_fusion
  148.8 80.6 %reduce-scatter.8.cloned.1.call-done = f32[16,256]{1,0:T(8,128)} async-done(((f32[512,256]{1,0:T(8,128)}), f32[16,256]{1,0:T(8,128)}) %reduce-scatter.8.cloned.1.call-update) | async-done | bytes 16400 | tf_op jit(solution)/shard_map/reduce_scatter | solution.py:90
  229.4 0.7 multiply_reduce_fusion.1
  230.1 25.9 %all-gather.3 = f32[32,1,256]{2,1,0:T(1,128)S(1)} all-gather(f32[1,1,256]{2,1,0:T(1,128)S(1)} %bitcast.70), channel_id=3, replica_groups=mesh['leaf'=16,'sep'=8,'mode'=2] {'leaf','mode'}, dimensions={0}, use_global_device_ids=true | all-gather | bytes 33792 | tf_op jit(solution)/shard_map/all_gather | solution.py:96
  256.2 0.9 convolution_convert_fusion.4
  257.0 22.7 %all_gather.21 = bf16[512,256]{1,0:T(8,128)(2,1)S(1)} all-gather(bf16[16,256]{1,0:T(8,128)(2,1)S(1)} %convolution_convert_fusion.4), channel_id=1, replica_groups=mesh['leaf'=16,'sep'=8,'mode'=2] {'leaf','mode'}, dimensions={0}, use_global_device_ids=true | all-gather | bytes 270336 | tf_op jit(solution)/shard_map/all_gather | solution.py:69
  279.7 85.1 %while.27 = (s32[]{:T(128)}, f32[512,256]{0,1:T(8,128)S(1)}, s32[16]{0:T(128)S(1)}, bf16[16,128,256]{2,1,0:T(8,128)(2,1)S(1)}, bf16[512,256]{1,0:T(8,128)(2,1)S(1)}, /*index=5*/s32[]{:T(128)}, s32[]{:T(128)}, s32[]{:T(128)}) while((s32[]{:T(128)}, f32[512,256]{0,1:T(8,128)S(1)}, s32[16]{0:T(128)S(1)}, bf16[16,128,256]{2,1,0:T(8,128)(2,1)S(1)}, ...), condition=%wide.region_9.10_spmd, body=%wide.region_8.9_spmd.sunk | while | flops 33652740 | bytes 2884751 | solution.py:65
  283.1 1.8 dynamic_update_slice.17
  288.3 1.9 dynamic_update_slice.17
  293.6 1.9 dynamic_update_slice.17
  298.8 1.9 dynamic_update_slice.17
  304.1 1.8 dynamic_update_slice.17
  309.3 1.9 dynamic_update_slice.17
  314.6 2.2 dynamic_update_slice.17
  320.2 1.9 dynamic_update_slice.17
  325.5 1.8 dynamic_update_slice.17
  330.7 1.9 dynamic_update_slice.17
  335.9 2.2 dynamic_update_slice.17
  341.5 1.9 dynamic_update_slice.17
  346.8 1.8 dynamic_update_slice.17
  352.0 1.9 dynamic_update_slice.17
  357.3 2.2 dynamic_update_slice.17
  362.9 1.9 dynamic_update_slice.17
  365.1 1.0 copy.34
  366.1 81.9 %reduce-scatter.10.cloned.1.call-done = f32[16,256]{1,0:T(8,128)} async-done(((f32[512,256]{1,0:T(8,128)}), f32[16,256]{1,0:T(8,128)}) %reduce-scatter.10.cloned.1.call-update) | async-done | bytes 16400
  448.0 0.8 copy.35
  449.0 25.9 %all-gather.4 = f32[32,1,256]{2,1,0:T(1,128)S(1)} all-gather(f32[1,1,256]{2,1,0:T(1,128)S(1)} %bitcast.69), channel_id=4, replica_groups=mesh['leaf'=16,'sep'=8,'mode'=2] {'leaf','mode'}, dimensions={0}, use_global_device_ids=true | all-gather | bytes 33792 | tf_op jit(solution)/shard_map/all_gather | solution.py:96
  475.0 0.9 fusion.17
  (141 shorter events, 35.5 us)
Async XLA Ops:
  7.2 140.5 %copy-start = (bf16[1,512,16]{1,2,0:T(8,128)(2,1)S(1)}, bf16[1,512,16]{1,2,0:T(8,128)(2,1)}, u32[]{:S(2)}) copy-start(bf16[1,512,16]{1,2,0:T(8,128)(2,1)} %param.17) | copy-start | bytes 49156
  7.2 6.3 %copy-start.4 = (s32[8,1]{0,1:T(1,128)S(1)}, s32[8,1]{0,1:T(1,128)}, u32[]{:S(2)}) copy-start(s32[8,1]{0,1:T(1,128)} %param.15) | copy-start | bytes 100
  7.2 6.5 %copy-start.5 = (s32[8]{0:T(128)S(1)}, s32[8]{0:T(128)}, u32[]{:S(2)}) copy-start(s32[8]{0:T(128)} %param.16) | copy-start | bytes 100
  7.2 16.3 %copy-start.2 = (f32[8,128]{1,0:T(8,128)S(1)}, f32[8,128]{1,0:T(8,128)}, u32[]{:S(2)}) copy-start(f32[8,128]{1,0:T(8,128)} %param.14) | copy-start | bytes 12292
  7.2 25.6 %reduce-scatter.6.cloned.1.call-start = ((), (), s32[]{:S(2)}) async-start(), calls=%async_computation.5 | async-start | bytes 3145728 | tf_op jit(solution)/shard_map/reduce_scatter | solution.py:13
  14.5 22.9 %all-to-all-start = ((s32[8,1,2]{2,1,0:T(1,128)}), s32[8,1,2]{2,1,0:T(1,128)S(1)}, u32[]{:S(2)}, u32[]{:S(2)}) async-start(s32[8,1,2]{2,1,0:T(1,128)} %bitcast.7), calls=%async_computation | async-start | bytes 8192 | tf_op jit(solution)/shard_map/all_to_all | solution.py:40
  34.5 9.6 %copy-start.1 = (bf16[1,16,256]{2,1,0:T(8,128)(2,1)S(1)}, bf16[1,16,256]{2,1,0:T(8,128)(2,1)}, u32[]{:S(2)}) copy-start(bf16[1,16,256]{2,1,0:T(8,128)(2,1)} %param.18) | copy-start | bytes 24580
  37.3 36.0 %all-to-all-start.1 = ((bf16[8,2,128,256]{3,1,2,0:T(2,128)(2,1)}), bf16[8,2,128,256]{3,1,2,0:T(2,128)(2,1)S(1)}, u32[]{:S(2)}, u32[]{:S(2)}) async-start(bf16[8,2,128,256]{3,1,2,0:T(2,128)(2,1)} %copy.30), calls=%async_computation.2 | async-start | bytes 2097152 | tf_op jit(solution)/shard_map/all_to_all | solution.py:37
  44.1 185.3 %reduce-scatter.8.cloned.1.call-start = ((), (), s32[]{:S(2)}) async-start(), calls=%async_computation.6 | async-start | bytes 540672 | tf_op jit(solution)/shard_map/reduce_scatter | solution.py:90
  73.6 182.6 %copy-start.3 = (bf16[1,2,256,256]{3,2,1,0:T(8,128)(2,1)S(1)}, bf16[1,2,256,256]{3,2,1,0:T(8,128)(2,1)}, u32[]{:S(2)}) copy-start(bf16[1,2,256,256]{3,2,1,0:T(8,128)(2,1)} %param.19) | copy-start | bytes 786436
  148.7 299.3 %reduce-scatter.10.cloned.1.call-start = ((), (), s32[]{:S(2)}) async-start(), calls=%async_computation.7 | async-start | bytes 540672
Sparse Core Ops, SparseCore 0:
  13.6 19.1 reduce-scatter.5
  148.9 80.5 reduce-scatter.7
  366.2 81.7 reduce-scatter.9
